TPU v7x, 128 devices: a whole 4x4x4 slice. The times are simulated.
128 devices in a mesh: au: 8 (over z_hi, y), pa: 8 (over x, z_lo), dev: 2 (over core).
Axes of the slice: x: 4, y: 4, z: 4 (z_hi: 2, z_lo: 2; z = z_hi * 2 + z_lo), core: 2. Of those that a mesh axis runs over, the one named last changes fastest.
Arguments:
- features: bfloat16 [8192, 64, 256], P('au', 'pa'), may hold values from -6 to 6
- item_ids: int32 [8192, 64], P('au', 'pa'), may hold values from 0 to 4095
- item_table: bfloat16 [4096, 256], replicated, may hold values from -4 to 4
- lengths: int32 [8192], P('au'), may hold values from 1 to 64
- routing_seed: int32 [4, 64], replicated, may hold values from 0 to 15
- w_qkv: bfloat16 [3, 256, 256], P(None, None, 'dev'), may hold values from -0.375 to 0.375
- w_out: bfloat16 [256, 256], P('dev'), may hold values from -0.375 to 0.375
- w_bilinear: bfloat16 [256, 256], P(None, 'dev'), may hold values from -0.375 to 0.375
- w_up: bfloat16 [256, 1024], P(None, 'dev'), may hold values from -0.375 to 0.375
- w_down: bfloat16 [1024, 256], P('dev'), may hold values from -0.1875 to 0.1875
Outputs:
- capsules: float32 [8192, 4, 256], P(('au', 'pa'), None, 'dev')
All inputs are finite; a program needn't handle non-finite values.
Results may differ from a plain program's by a relative error of at most 0.012.
The roundings to bfloat16 on the way count: a program that leaves them out, or rounds other values in their place, can miss the bound.
Values may be sent and summed in bfloat16 or wider, within the bound.
No kernel may reach another device: no remote copies, remote signals or barrier semaphores. Data moves between devices by JAX's collectives and lax.ppermute only.
A program may use at most 128 MiB of HBM per device.

v0:
```python
import jax
import jax.numpy as jnp
from jax import lax
from jax.sharding import PartitionSpec as P

D = 256
HEADS = 4
CAPS = 4
ITERS = 3


def laid_out(tiles, dim):
    tiles = jnp.moveaxis(tiles, 0, dim)
    shape = tiles.shape
    return tiles.reshape(*shape[:dim], shape[dim] * shape[dim + 1], *shape[dim + 2 :])


def gather_packed(arrays, axis, dims):
    vector = jnp.concatenate([a.reshape(-1) for a in arrays])
    lines, at, finished = (lax.all_gather(vector, axis), 0, [])
    for a, dim in zip(arrays, dims):
        tiles = lines[:, at : at + a.size].reshape(-1, *a.shape)
        finished.append(laid_out(tiles, dim))
        at += a.size
    return tuple(finished)


def local_routing(vectors, valid, base):
    user_count, history_len, width_here = vectors.shape
    logits = jnp.broadcast_to(base[None], (user_count, CAPS, history_len))
    capsules = jnp.zeros((user_count, CAPS, width_here), jnp.float32)
    for sweep in range(ITERS):
        weights = jax.nn.softmax(logits, axis=1) * valid[:, None, :]
        summed = jnp.einsum("ukl,uld->ukd", weights, vectors, precision=lax.Precision.HIGHEST)
        squares = jnp.sum(summed * summed, axis=-1)
        factor = jnp.sqrt(squares) / (1.0 + squares)
        capsules = summed * factor[..., None]
        if sweep + 1 < ITERS:
            logits = logits + jnp.einsum(
                "ukd,uld->ukl", capsules, vectors, precision=lax.Precision.HIGHEST
            )
    return capsules


def body(
    features, item_ids, item_table, lengths, routing_seed, w_qkv, w_out, w_bilinear, w_up, w_down
):
    pa_count = lax.axis_size("pa")
    dev_count = lax.axis_size("dev")
    owned_users = lengths.shape[0] // pa_count
    head_size = D // HEADS
    share = owned_users // dev_count
    core = lax.axis_index("dev")

    def pick(array):
        shaped = array.reshape((pa_count, dev_count, share) + array.shape[1:])
        chosen = lax.dynamic_index_in_dim(shaped, core, 1, keepdims=False)
        return chosen.reshape((pa_count * share,) + array.shape[1:])

    features = pick(features)
    item_ids = pick(item_ids)
    lengths = pick(lengths)
    w_qkv, w_out, w_bilinear, w_up, w_down = gather_packed(
        (w_qkv, w_out, w_bilinear, w_up, w_down), "dev", (2, 0, 1, 1, 0)
    )
    own_lens = lax.dynamic_slice_in_dim(lengths, lax.axis_index("pa") * share, share)
    features, item_ids = (
        lax.all_to_all(features, "pa", split_axis=0, concat_axis=1, tiled=True),
        lax.all_to_all(item_ids, "pa", split_axis=0, concat_axis=1, tiled=True),
    )
    user_count, span_here, model_width = features.shape
    heads_here = w_qkv.shape[2] // head_size
    inputs = (
        features.astype(jnp.float32) + jnp.take(item_table, item_ids, axis=0).astype(jnp.float32)
    ).astype(jnp.bfloat16)
    flat_rows = inputs.reshape(-1, model_width)

    def project(index):
        shaped = w_qkv[index].reshape(model_width, heads_here, head_size)
        made = jnp.einsum(
            "nd,dhe->hne", flat_rows, shaped, preferred_element_type=jnp.float32
        ).astype(jnp.bfloat16)
        return made.reshape(heads_here, user_count, span_here, head_size)

    queries = project(0)
    key_block = project(1)
    value_block = project(2)
    score_scale = 1.0 / head_size**0.5
    count_here = key_block.shape[2]
    scores = (
        jnp.einsum("huqe,huke->huqk", queries, key_block, preferred_element_type=jnp.float32)
        * score_scale
    )
    positions = jnp.arange(count_here, dtype=jnp.int32)
    valid_keys = positions[None, :] < own_lens[:, None]
    mask_four = valid_keys[None, :, None, :]
    probs = jnp.where(mask_four, jnp.exp(scores), 0.0)
    totals = jnp.sum(probs, axis=-1)
    weighted = jnp.einsum(
        "huqk,huke->huqe",
        probs.astype(jnp.bfloat16),
        value_block,
        preferred_element_type=jnp.float32,
    )
    attended = (weighted / totals[..., None]).astype(jnp.bfloat16)
    out_heads = w_out.reshape(heads_here, head_size, w_out.shape[1])
    attended_term = jnp.einsum(
        "huqe,hef->uqf", attended, out_heads, preferred_element_type=jnp.float32
    )
    hidden = jax.nn.gelu(jnp.dot(flat_rows, w_up, preferred_element_type=jnp.float32)).astype(
        jnp.bfloat16
    )
    partial_terms = attended_term.reshape(-1, w_out.shape[1]) + jnp.dot(
        hidden, w_down, preferred_element_type=jnp.float32
    )
    interest_in = (
        partial_terms + jnp.dot(flat_rows, w_bilinear, preferred_element_type=jnp.float32)
    ).astype(jnp.bfloat16)
    interest_in = interest_in.reshape(user_count, span_here, -1)
    history_len = interest_in.shape[1]
    valid = (jnp.arange(history_len)[None, :] < own_lens[:, None]).astype(jnp.float32)
    base = (routing_seed.astype(jnp.float32) - 7.5) * 0.25
    routed = local_routing(interest_in.astype(jnp.float32), valid, base)
    capsules = lax.all_to_all(routed, "dev", split_axis=2, concat_axis=0, tiled=True)
    return capsules


def solution(mesh):
    in_specs = (
        P("au", "pa", None),
        P("au", "pa"),
        P(),
        P("au"),
        P(),
        P(None, None, "dev"),
        P("dev", None),
        P(None, "dev"),
        P(None, "dev"),
        P("dev", None),
    )
    out_specs = P(("au", "pa"), None, "dev")
    return jax.shard_map(body, mesh=mesh, in_specs=in_specs, out_specs=out_specs, check_vma=False)
```

profile of v0, /device:TPU:1, one launch (start us, length us, event | category | flops | bytes accessed | tf_op | source)
XLA Modules:
  0.0 140.4 jit_solution(1867006073911560895)
XLA Ops:
  14.3 6.2 %all-to-all-start.1 = ((s32[8,1,512]{2,1,0:T(1,128)}), s32[8,1,512]{2,1,0:T(1,128)S(1)}, u32[]{:S(2)}, u32[]{:S(2)}) async-start(s32[8,1,512]{2,1,0:T(1,128)} %reshape.245), calls=%async_computation.1 | async-start | bytes 32768 | tf_op jit(solution)/shard_map/all_to_all | solution.py:69
  21.5 3.0 %constant_dynamic-slice_fusion.1 = bf16[8,1,64,8,256]{4,3,2,1,0:T(8,128)(2,1)} fusion(bf16[8,2,64,8,256]{4,3,2,1,0:T(8,128)(2,1)} %bitcast.141, s32[]{:T(128)S(6)} %select_n.42), kind=kLoop, calls=%fused_computation.91 | loop fusion | bytes 4194308 | tf_op jit(solution)/shard_map/jit(dynamic_index_in_dim)/dynamic_slice | solution.py:57
  25.6 4.3 %all-to-all-start = ((bf16[512,8,256]{2,1,0:T(8,128)(2,1)}), bf16[512,8,256]{2,1,0:T(8,128)(2,1)}, u32[]{:S(2)}, u32[]{:S(2)}) async-start(bf16[512,8,256]{2,1,0:T(8,128)(2,1)} %bitcast.131), calls=%async_computation | async-start | bytes 4194304 | tf_op jit(solution)/shard_map/all_to_all | solution.py:68
  31.6 16.9 %gather_fusion = bf16[4096,256]{1,0:T(8,128)(2,1)} fusion(bf16[4096,256]{1,0:T(8,128)(2,1)S(1)} %copy-done, s32[4096]{0:T(1024)S(1)} %broadcast_clamp_fusion), kind=kCustom, calls=%fused_computation | custom fusion | bytes 4210688 | tf_op jit(solution)/shard_map/jit(_take)/gather | solution.py:74
  48.5 1.9 %reshape.233 = bf16[2,425984]{1,0:T(2,128)(2,1)S(1)} reshape(bf16[851968]{0:T(1024)(128)(2,1)} %all-gather.3.cloned.1.call-done) | data formatting | bytes 3407872 | tf_op jit(solution)/shard_map/all_gather | solution.py:20
  51.6 1.6 %fusion.67 = (bf16[2,131072]{1,0:T(2,128)(2,1)}, bf16[2,131072]{1,0:T(2,128)(2,1)S(1)}) fusion(bf16[2,425984]{1,0:T(2,128)(2,1)S(1)} %reshape.233), kind=kLoop, calls=%fused_computation.100 | loop fusion | bytes 2097152 | tf_op jit(solution)/shard_map/slice | solution.py:22
  56.3 1.8 %slice_bitcast_fusion.1 = (bf16[1,2,256,128]{3,1,2,0:T(2,128)(2,1)}, bf16[2,32768]{1,0:T(2,128)(2,1)S(1)}) fusion(bf16[2,425984]{1,0:T(2,128)(2,1)} %copy-done.5), kind=kLoop, calls=%fused_computation.51 | loop fusion | bytes 524288
  62.5 3.0 %fusion.27 = bf16[64,8,8,256]{3,2,0,1:T(8,128)(2,1)S(1)} fusion(bf16[8,64,8,256]{3,2,1,0:T(8,128)(2,1)} %bitcast.36, bf16[64,8,8,256]{3,2,1,0:T(8,128)(2,1)S(1)} %bitcast.130, pred[64,8,8]{2,0,1:T(8,128)(4,1)S(1)} %copy.106), kind=kLoop, calls=%fused_computation.32 | loop fusion | flops 5242880 | bytes 6295552 | tf_op jit(solution)/shard_map/convert_element_type | solution.py:75
  65.8 2.1 %fusion.22 = bf16[4,4096,64]{1,2,0:T(8,128)(2,1)} fusion(bf16[256,4,64]{0,2,1:T(8,128)(2,1)S(1)} %bitcast.147, bf16[4096,256,1]{1,0,2:T(8,128)(2,1)S(1)} %bitcast.125), kind=kOutput, calls=%fused_computation.27 | convolution fusion | flops 537919488 | bytes 4325376 | tf_op jit(solution)/shard_map/nd,dhe->hne/dot_general | solution.py:80
  67.9 4.8 %copy.133 = bf16[4,4096,64]{2,1,0:T(8,128)(2,1)} copy(bf16[4,4096,64]{1,2,0:T(8,128)(2,1)} %fusion.22) | data formatting | bytes 4194304 | tf_op jit(solution)/shard_map/reshape | solution.py:83
  72.7 2.1 %fusion.21 = bf16[4,4096,64]{1,2,0:T(8,128)(2,1)} fusion(bf16[256,4,64]{0,2,1:T(8,128)(2,1)S(1)} %bitcast.146, bf16[4096,256,1]{1,0,2:T(8,128)(2,1)S(1)} %bitcast.126), kind=kOutput, calls=%fused_computation.26 | convolution fusion | flops 537919488 | bytes 4325376 | tf_op jit(solution)/shard_map/nd,dhe->hne/dot_general | solution.py:80
  74.9 4.8 %copy.132 = bf16[4,4096,64]{2,1,0:T(8,128)(2,1)} copy(bf16[4,4096,64]{1,2,0:T(8,128)(2,1)} %fusion.21) | data formatting | bytes 4194304 | tf_op jit(solution)/shard_map/reshape | solution.py:83
  79.6 2.1 %fusion.23 = bf16[4,4096,64]{1,2,0:T(8,128)(2,1)} fusion(bf16[256,4,64]{0,2,1:T(8,128)(2,1)S(1)} %bitcast.145, bf16[4096,256,1]{1,0,2:T(8,128)(2,1)S(1)} %bitcast.127), kind=kOutput, calls=%fused_computation.28 | convolution fusion | flops 537919488 | bytes 4325376 | tf_op jit(solution)/shard_map/nd,dhe->hne/dot_general | solution.py:80
  81.7 4.8 %copy.134 = bf16[4,4096,64]{2,1,0:T(8,128)(2,1)} copy(bf16[4,4096,64]{1,2,0:T(8,128)(2,1)} %fusion.23) | data formatting | bytes 4194304 | tf_op jit(solution)/shard_map/reshape | solution.py:83
  86.6 5.0 %fusion.13 = (f32[4,64,64]{2,1,0:T(8,128)S(1)}, f32[4,64,64,64]{2,3,1,0:T(8,128)S(1)}) fusion(pred[64,64]{1,0:T(8,128)(4,1)S(1)} %get-tuple-element.15, bf16[4,64,64,64]{3,2,1,0:T(8,128)(2,1)} %bitcast.134, bf16[4,64,64,64]{3,2,1,0:T(8,128)(2,1)} %bitcast.133), kind=kOutput, calls=%fused_computation.16 | convolution fusion | flops 137347072 | bytes 8458240 | tf_op jit(solution)/shard_map/huqe,huke->huqk/dot_general | solution.py:91
  91.5 5.3 %fusion.10 = bf16[64,64,64,4]{2,1,0,3:T(8,128)(2,1)S(1)} fusion(f32[64,64,4]{1,0,2:T(8,128)S(1)} %bitcast.156, bf16[4,64,64,64]{3,2,1,0:T(8,128)(2,1)S(1)} %bitcast.135, f32[4,64,64,64]{2,3,1,0:T(8,128)S(1)} %get-tuple-element.17, pred[64,64]{1,0:T(8,128)(4,1)S(1)} %get-tuple-element.15), kind=kOutput, calls=%fused_computation.13 | convolution fusion | flops 139460608 | bytes 8458240 | tf_op jit(solution)/shard_map/huqk,huke->huqe/dot_general | solution.py:99
  96.8 2.8 %convolution_bitcast_fusion = f32[4096,256]{1,0:T(8,128)} fusion(bf16[4096,64,4]{1,0,2:T(8,128)(2,1)S(1)} %bitcast.132, bf16[4,64,256]{2,1,0:T(8,128)(2,1)S(1)} %reshape_reshape_reshape.3), kind=kOutput, calls=%fused_computation.19 | convolution fusion | flops 536870912 | bytes 6422528 | tf_op jit(solution)/shard_map/huqe,hef->uqf/dot_general | solution.py:107
  99.7 9.4 %fusion.15 = f32[4096,256]{1,0:T(8,128)} fusion(f32[4096,256]{1,0:T(8,128)} %convolution_bitcast_fusion, bf16[1024,256]{1,0:T(8,128)(2,1)} %reshape_reshape.3, bf16[4096,256]{1,0:T(8,128)(2,1)S(1)} %bitcast.128, bf16[256,1024]{0,1:T(8,128)(2,1)S(1)} %bitcast.148), kind=kOutput, calls=%fused_computation.20 | convolution fusion | flops 4333764608 | bytes 11534336 | tf_op jit(solution)/shard_map/dot_general | solution.py:113
  109.0 3.6 %fusion.20 = bf16[4096,256]{1,0:T(8,128)(2,1)S(1)} fusion(f32[4096,256]{1,0:T(8,128)} %fusion.15, bf16[4096,256]{1,0:T(8,128)(2,1)} %bitcast.129, bf16[256,256]{0,1:T(8,128)(2,1)S(1)} %bitcast.144), kind=kOutput, calls=%fused_computation.22 | convolution fusion | flops 538968064 | bytes 8519680 | tf_op jit(solution)/shard_map/dot_general | solution.py:117
  113.9 1.8 %convolution_add_fusion.2 = f32[64,4,64]{2,1,0:T(4,128)S(1)} fusion(bf16[64,64,256]{2,1,0:T(8,128)(2,1)S(1)} %bitcast.121, f32[64,4,256]{2,1,0:T(4,128)S(1)} %get-tuple-element.19, f32[64,4]{1,0:T(8,128)S(1)} %copy.121, f32[4,64]{1,0:T(4,128)S(1)} %get-tuple-element.12), kind=kOutput, calls=%fused_computation.40 | convolution fusion | flops 50413568 | bytes 2426880 | tf_op jit(solution)/shard_map/ukd,uld->ukl/dot_general | solution.py:39
  117.1 3.5 %convolution_add_fusion.1 = f32[64,4,64]{2,1,0:T(4,128)S(1)} fusion(f32[64,4,64]{2,1,0:T(4,128)S(1)} %convolution_add_fusion.2, bf16[64,64,256]{2,1,0:T(8,128)(2,1)} %bitcast.123, f32[64,4,256]{2,1,0:T(4,128)S(1)} %get-tuple-element.23, f32[64,4]{1,0:T(8,128)S(1)} %copy.124), kind=kOutput, calls=%fused_computation.39 | convolution fusion | flops 50413568 | bytes 2491392 | tf_op jit(solution)/shard_map/ukd,uld->ukl/dot_general | solution.py:39
  120.8 2.6 %multiply_reduce_fusion = (f32[64,4]{1,0:T(8,128)S(1)}, f32[64,4,256]{2,1,0:T(4,128)S(1)}) fusion(bf16[64,64,256]{2,1,0:T(8,128)(2,1)} %bitcast.124, f32[64,4,64]{2,1,0:T(4,128)S(1)} %get-tuple-element.25, f32[64,64]{1,0:T(8,128)S(1)} %get-tuple-element.24, f32[64,64]{1,0:T(8,128)S(1)} %get-tuple-element.14), kind=kOutput, calls=%fused_computation.45 | convolution fusion | flops 50495232 | bytes 2458624 | tf_op jit(solution)/shard_map/ukl,uld->ukd/dot_general | solution.py:34
  124.6 5.7 %all_to_all.46 = f32[2,1,32768]{2,1,0:T(1,128)S(1)} all-to-all(f32[2,1,32768]{2,1,0:T(1,128)S(1)} %reshape.247), channel_id=1, replica_groups=mesh['au'=8,'pa'=8,'dev'=2] {'dev'}, dimensions={0} | all-to-all | bytes 524288 | tf_op jit(solution)/shard_map/all_to_all | solution.py:124
  130.8 1.4 %reduce.8 = f32[2,32768]{1,0:T(2,128)S(1)} reduce(f32[2,1,32768]{2,1,0:T(1,128)S(1)} %all_to_all.46, f32[]{:T(128)} %broadcast.111), dimensions={1}, to_apply=%all_to_all.39.reduce_sub_computation | reduce | bytes 524292 | tf_op jit(solution)/shard_map/all_to_all | solution.py:124
  (89 shorter events, 26.0 us)
Async XLA Ops:
  6.5 25.0 %copy-start = (bf16[4096,256]{1,0:T(8,128)(2,1)S(1)}, bf16[4096,256]{1,0:T(8,128)(2,1)}, u32[]{:S(2)}) copy-start(bf16[4096,256]{1,0:T(8,128)(2,1)} %param.12) | copy-start | bytes 6291460
  6.5 18.0 %copy-start.11 = (s32[4,64]{1,0:T(4,128)S(1)}, s32[4,64]{1,0:T(4,128)}, u32[]{:S(2)}) copy-start(s32[4,64]{1,0:T(4,128)} %param.14) | copy-start | bytes 3076
  6.5 42.0 %all-gather.3.cloned.1.call-start = ((), (), s32[]{:S(2)}) async-start(), calls=%async_computation.3 | async-start | bytes 2555904 | tf_op jit(solution)/shard_map/all_gather | solution.py:20
  11.7 1.0 copy-start.7
  14.3 11.2 %all-to-all-start.1 = ((s32[8,1,512]{2,1,0:T(1,128)}), s32[8,1,512]{2,1,0:T(1,128)S(1)}, u32[]{:S(2)}, u32[]{:S(2)}) async-start(s32[8,1,512]{2,1,0:T(1,128)} %reshape.245), calls=%async_computation.1 | async-start | bytes 32768 | tf_op jit(solution)/shard_map/all_to_all | solution.py:69
  25.6 36.9 %all-to-all-start = ((bf16[512,8,256]{2,1,0:T(8,128)(2,1)}), bf16[512,8,256]{2,1,0:T(8,128)(2,1)}, u32[]{:S(2)}, u32[]{:S(2)}) async-start(bf16[512,8,256]{2,1,0:T(8,128)(2,1)} %bitcast.131), calls=%async_computation | async-start | bytes 4194304 | tf_op jit(solution)/shard_map/all_to_all | solution.py:68
  50.4 1.2 copy-start.5
  53.1 9.3 %copy-start.4 = (bf16[4096,256]{1,0:T(8,128)(2,1)S(1)}, bf16[4096,256]{1,0:T(8,128)(2,1)}, u32[]{:S(2)}) copy-start(bf16[4096,256]{1,0:T(8,128)(2,1)} %gather_fusion) | copy-start | bytes 6291460
  62.5 3.3 %copy-start.9 = (bf16[1,256,2,128]{1,3,2,0:T(8,128)(2,1)S(1)}, bf16[1,256,2,128]{1,3,2,0:T(8,128)(2,1)}, u32[]{:S(2)}) copy-start(bf16[1,256,2,128]{1,3,2,0:T(8,128)(2,1)} %copy.110) | copy-start | bytes 393220
  65.8 33.8 %copy-start.3 = (bf16[64,8,8,256]{3,2,1,0:T(8,128)(2,1)}, bf16[64,8,8,256]{3,2,1,0:T(8,128)(2,1)S(1)}, u32[]{:S(2)}) copy-start(bf16[64,8,8,256]{3,2,1,0:T(8,128)(2,1)S(1)} %copy.109) | copy-start | bytes 6291460
  67.9 4.8 %copy-start.8 = (bf16[1,256,2,128]{1,3,2,0:T(8,128)(2,1)S(1)}, bf16[1,256,2,128]{1,3,2,0:T(8,128)(2,1)}, u32[]{:S(2)}) copy-start(bf16[1,256,2,128]{1,3,2,0:T(8,128)(2,1)} %copy.103) | copy-start | bytes 393220
  86.6 5.0 %copy-start.6 = (bf16[4,4096,64]{2,1,0:T(8,128)(2,1)S(1)}, bf16[4,4096,64]{2,1,0:T(8,128)(2,1)}, u32[]{:S(2)}) copy-start(bf16[4,4096,64]{2,1,0:T(8,128)(2,1)} %copy.134) | copy-start | bytes 6291460
  96.8 2.9 %copy-start.10 = (bf16[256,2,512]{0,2,1:T(8,128)(2,1)S(1)}, bf16[256,2,512]{0,2,1:T(8,128)(2,1)}, u32[]{:S(2)}) copy-start(bf16[256,2,512]{0,2,1:T(8,128)(2,1)} %copy.117) | copy-start | bytes 1572868
  112.6 3.2 %copy-start.2 = (bf16[4096,256]{1,0:T(8,128)(2,1)}, bf16[4096,256]{1,0:T(8,128)(2,1)S(1)}, u32[]{:S(2)}) copy-start(bf16[4096,256]{1,0:T(8,128)(2,1)S(1)} %fusion.20) | copy-start | bytes 6291460
  117.1 16.5 %copy-start.1 = (bf16[4096,256]{1,0:T(8,128)(2,1)S(1)}, bf16[4096,256]{1,0:T(8,128)(2,1)}, u32[]{:S(2)}) copy-start(bf16[4096,256]{1,0:T(8,128)(2,1)} %param.12) | copy-start | bytes 6291460
Sparse Core Ops, SparseCore 0:
  12.8 16.3 all-gather.2
where the time goes:
time: 141 us; the launch traced here: 140 us
  local copies, waits for them, and re-layouts  61.2 us (43%)
  matrix products  42.4 us (30%)
  between operations  13.8 us (10%)
  starting transfers between devices  10.5 us (7%)
  other arithmetic  5.86 us (4%)
  blocking collectives  5.69 us (4%)
    gather x1, local copies, waits for them, and re-layouts, body(): jnp.take(item_table, item_ids, axis=0).astype(jnp.float32)  16.9 us
    reshape x3, local copies, waits for them, and re-layouts, project(): return made.reshape(heads_here, user_count, span_here, head_size)  14.4 us
    unnamed x40, local copies, waits for them, and re-layouts  14.3 us
    dot_general x1, matrix products, body(): jnp.dot(hidden, w_down, preferred_element_type=jnp.float32)  9.38 us
    dot_general x3, matrix products, project(): jnp.einsum('nd,dhe->hne', flat_rows, shaped, preferred_element_type=jnp.f...  6.29 us
    all_to_all x1, starting transfers between devices, body(): lax.all_to_all(item_ids, 'pa', split_axis=0, concat_axis=1, tiled=True)  6.2 us
    all_to_all x1, blocking collectives, body(): lax.all_to_all(routed, 'dev', split_axis=2, concat_axis=0, tiled=True)  5.69 us
    dot_general x2, matrix products, local_routing(): jnp.einsum('ukd,uld->ukl', capsules, vectors, precision=lax.Precision.HIG...  5.34 us
  transfers between devices with their start and end apart: 3, of which 1 were waited for; matrix products, arithmetic and copies ran while one was open for 26% of the time, Pallas kernels for 0%

commit v1 on v0

--- a/solution.py
+++ b/solution.py
@@ -7,6 +7,15 @@
 HEADS = 4
 CAPS = 4
 ITERS = 3
+cells_replace = lambda lane_axis, array_here: jnp.concatenate(
+    lax.all_to_all(
+        jnp.stack(jnp.split(array_here, lax.axis_size(lane_axis), axis=0), axis=0),
+        axis_name=lane_axis,
+        split_axis=0,
+        concat_axis=0,
+    ),
+    axis=1,
+)
 
 
 def laid_out(tiles, dim):
@@ -65,7 +74,7 @@
     )
     own_lens = lax.dynamic_slice_in_dim(lengths, lax.axis_index("pa") * share, share)
     features, item_ids = (
-        lax.all_to_all(features, "pa", split_axis=0, concat_axis=1, tiled=True),
+        cells_replace("pa", array_here=features),
         lax.all_to_all(item_ids, "pa", split_axis=0, concat_axis=1, tiled=True),
     )
     user_count, span_here, model_width = features.shape

time: 141 us -> 144 us (1.021)
  matrix products: 42.4 us -> 38.9 us
  local copies, waits for them, and re-layouts: 61.2 us -> 64.7 us
  waiting for transfers between devices: 0.95 us -> 3.22 us
    unnamed x40 -> x41, local copies, waits for them, and re-layouts: 14.3 us -> 20 us
    all_to_all x1, waiting for transfers between devices: 0.01 us -> 3.2 us  [lax.all_to_all(jnp.stack(jnp.split(array_here, lax.axis_size(lane_axis),...]
    dynamic_slice x4 -> x3, local copies, waits for them, and re-layouts: 3.08 us -> 0.06 us  [pick(): chosen = lax.dynamic_index_in_dim(shaped, core, 1, keepdims=False)]
    dot_general x2, matrix products: 5.34 us -> 3.61 us  [local_routing(): jnp.einsum('ukd,uld->ukl', capsules, vectors, precision=lax.Precision.HIG...]
    another operation x0 -> x1, local copies, waits for them, and re-layouts: none -> 1.7 us  [jnp.stack(jnp.split(array_here, lax.axis_size(lane_axis), axis=0), axis=0)]
    dot_general x3, matrix products: 4.73 us -> 3.14 us  [local_routing(): jnp.einsum('ukl,uld->ukd', weights, vectors, precision=lax.Precision.HIGH...]
    slice x4, local copies, waits for them, and re-layouts: 1.66 us -> 3.21 us  [project(): shaped = w_qkv[index].reshape(model_width, heads_here, head_size)]
  transfers between devices with their start and end apart: 3 -> 3, of which waited for: 1 -> 1; matrix products, arithmetic and copies ran while one was open for 26% -> 32% of each run, Pallas kernels for 0% -> 0%
where the time goes in v1:
time: 144 us; the launch traced here: 143 us
  local copies, waits for them, and re-layouts  64.7 us (45%)
  matrix products  38.9 us (27%)
  between operations  13.7 us (10%)
  starting transfers between devices  11.3 us (8%)
  other arithmetic  5.57 us (4%)
  blocking collectives  5.49 us (4%)
  waiting for transfers between devices  3.22 us (2%)
    unnamed x41, local copies, waits for them, and re-layouts  20 us
    gather x1, local copies, waits for them, and re-layouts, body(): jnp.take(item_table, item_ids, axis=0).astype(jnp.float32)  16.9 us
    reshape x3, local copies, waits for them, and re-layouts, project(): return made.reshape(heads_here, user_count, span_here, head_size)  14.4 us
    dot_general x1, matrix products, body(): jnp.dot(hidden, w_down, preferred_element_type=jnp.float32)  9.2 us
    dot_general x3, matrix products, project(): jnp.einsum('nd,dhe->hne', flat_rows, shaped, preferred_element_type=jnp.f...  6.29 us
    all_to_all x1, starting transfers between devices, body(): lax.all_to_all(item_ids, 'pa', split_axis=0, concat_axis=1, tiled=True)  6.2 us
    all_to_all x1, blocking collectives, body(): lax.all_to_all(routed, 'dev', split_axis=2, concat_axis=0, tiled=True)  5.49 us
    dot_general x1, matrix products, body(): jnp.einsum('huqk,huke->huqe', probs.astype(jnp.bfloat16), value_block, pr...  5.27 us
  transfers between devices with their start and end apart: 3, of which 1 were waited for; matrix products, arithmetic and copies ran while one was open for 32% of the time, Pallas kernels for 0%

profile of v1, /device:TPU:1, one launch (start us, length us, event | category | flops | bytes accessed | tf_op | source)
XLA Modules:
  0.0 142.9 jit_solution(12511521837547818165)
XLA Ops:
  8.3 6.2 %all-to-all-start.1 = ((s32[8,1,512]{2,1,0:T(1,128)}), s32[8,1,512]{2,1,0:T(1,128)S(1)}, u32[]{:S(2)}, u32[]{:S(2)}) async-start(s32[8,1,512]{2,1,0:T(1,128)} %reshape.257), calls=%async_computation.1 | async-start | bytes 32768 | tf_op jit(solution)/shard_map/all_to_all | solution.py:78
  25.8 1.7 %fusion.40 = bf16[8,64,8,256]{3,2,1,0:T(8,128)(2,1)} fusion(bf16[8,64,8,256]{3,2,1,0:T(8,128)(2,1)} %fusion.41, bf16[8,2,64,8,256]{4,3,2,1,0:T(8,128)(2,1)} %bitcast.168, s32[]{:T(128)S(6)} %add.106, s32[]{:T(128)S(6)} %select_n.42), kind=kLoop, calls=%fused_computation.52 | loop fusion | bytes 524296
  29.2 1.7 %fusion.38 = bf16[8,64,8,256]{3,2,1,0:T(8,128)(2,1)} fusion(bf16[8,64,8,256]{3,2,1,0:T(8,128)(2,1)} %fusion.39, bf16[8,2,64,8,256]{4,3,2,1,0:T(8,128)(2,1)} %bitcast.170, s32[]{:T(128)S(6)} %add.108, s32[]{:T(128)S(6)} %select_n.42), kind=kLoop, calls=%fused_computation.48 | loop fusion | bytes 524296
  30.9 1.7 %fusion.37 = bf16[8,64,8,256]{3,2,1,0:T(8,128)(2,1)} fusion(bf16[8,64,8,256]{3,2,1,0:T(8,128)(2,1)} %fusion.38, bf16[8,2,64,8,256]{4,3,2,1,0:T(8,128)(2,1)} %bitcast.171, s32[]{:T(128)S(6)} %add.109, s32[]{:T(128)S(6)} %select_n.42), kind=kLoop, calls=%fused_computation.46 | loop fusion | bytes 524296
  32.6 1.7 %fusion.36 = bf16[8,64,8,256]{3,2,1,0:T(8,128)(2,1)} fusion(bf16[8,64,8,256]{3,2,1,0:T(8,128)(2,1)} %fusion.37, bf16[8,2,64,8,256]{4,3,2,1,0:T(8,128)(2,1)} %bitcast.172, s32[]{:T(128)S(6)} %add.110, s32[]{:T(128)S(6)} %select_n.42), kind=kLoop, calls=%fused_computation.44 | loop fusion | bytes 524296 | tf_op jit(solution)/shard_map/stack | solution.py:12
  34.4 5.1 %all-to-all-start = ((bf16[8,64,8,256]{3,2,1,0:T(8,128)(2,1)}), bf16[8,64,8,256]{3,2,1,0:T(8,128)(2,1)}, u32[]{:S(2)}, u32[]{:S(2)}) async-start(bf16[8,64,8,256]{3,2,1,0:T(8,128)(2,1)} %fusion.36), calls=%async_computation | async-start | bytes 4194304 | tf_op jit(solution)/shard_map/all_to_all | solution.py:11
  41.2 16.9 %gather_fusion = bf16[4096,256]{1,0:T(8,128)(2,1)} fusion(bf16[4096,256]{1,0:T(8,128)(2,1)S(1)} %copy-done, s32[4096]{0:T(1024)S(1)} %broadcast_clamp_fusion), kind=kCustom, calls=%fused_computation | custom fusion | bytes 4210688 | tf_op jit(solution)/shard_map/jit(_take)/gather | solution.py:83
  58.1 1.9 %reshape.245 = bf16[2,425984]{1,0:T(2,128)(2,1)S(1)} reshape(bf16[851968]{0:T(1024)(128)(2,1)} %all-gather.3.cloned.1.call-done) | data formatting | bytes 3407872 | tf_op jit(solution)/shard_map/all_gather | solution.py:29
  66.1 3.2 %all-to-all-done = bf16[8,64,8,256]{3,2,1,0:T(8,128)(2,1)} async-done(((bf16[8,64,8,256]{3,2,1,0:T(8,128)(2,1)}), bf16[8,64,8,256]{3,2,1,0:T(8,128)(2,1)}, u32[]{:S(2)}, u32[]{:S(2)}) %all-to-all-start) | async-done | bytes 2097184 | tf_op jit(solution)/shard_map/all_to_all | solution.py:11
  69.3 2.8 %fusion.26 = bf16[64,8,8,256]{3,2,1,0:T(8,128)(2,1)S(1)} fusion(bf16[8,64,8,256]{3,2,1,0:T(8,128)(2,1)} %all-to-all-done, bf16[64,8,8,256]{3,2,1,0:T(8,128)(2,1)} %bitcast.155, pred[64,8,8]{2,1,0:T(8,128)(4,1)S(1)} %copy.132), kind=kLoop, calls=%fused_computation.31 | loop fusion | flops 5242880 | bytes 6295552 | tf_op jit(solution)/shard_map/convert_element_type | solution.py:84
  72.1 2.1 %fusion.22 = bf16[4,4096,64]{1,2,0:T(8,128)(2,1)} fusion(bf16[256,4,64]{0,2,1:T(8,128)(2,1)S(1)} %bitcast.178, bf16[4096,256,1]{1,0,2:T(8,128)(2,1)S(1)} %bitcast.150), kind=kOutput, calls=%fused_computation.27 | convolution fusion | flops 537919488 | bytes 4325376 | tf_op jit(solution)/shard_map/nd,dhe->hne/dot_general | solution.py:89
  74.2 4.8 %copy.157 = bf16[4,4096,64]{2,1,0:T(8,128)(2,1)} copy(bf16[4,4096,64]{1,2,0:T(8,128)(2,1)} %fusion.22) | data formatting | bytes 4194304 | tf_op jit(solution)/shard_map/reshape | solution.py:92
  79.0 2.1 %fusion.21 = bf16[4,4096,64]{1,2,0:T(8,128)(2,1)} fusion(bf16[256,4,64]{0,2,1:T(8,128)(2,1)S(1)} %bitcast.177, bf16[4096,256,1]{1,0,2:T(8,128)(2,1)S(1)} %bitcast.151), kind=kOutput, calls=%fused_computation.26 | convolution fusion | flops 537919488 | bytes 4325376 | tf_op jit(solution)/shard_map/nd,dhe->hne/dot_general | solution.py:89
  81.1 4.8 %copy.156 = bf16[4,4096,64]{2,1,0:T(8,128)(2,1)} copy(bf16[4,4096,64]{1,2,0:T(8,128)(2,1)} %fusion.21) | data formatting | bytes 4194304 | tf_op jit(solution)/shard_map/reshape | solution.py:92
  85.9 2.1 %fusion.23 = bf16[4,4096,64]{1,2,0:T(8,128)(2,1)} fusion(bf16[256,4,64]{0,2,1:T(8,128)(2,1)S(1)} %bitcast.176, bf16[4096,256,1]{1,0,2:T(8,128)(2,1)S(1)} %bitcast.152), kind=kOutput, calls=%fused_computation.28 | convolution fusion | flops 537919488 | bytes 4325376 | tf_op jit(solution)/shard_map/nd,dhe->hne/dot_general | solution.py:89
  88.0 4.8 %copy.158 = bf16[4,4096,64]{2,1,0:T(8,128)(2,1)} copy(bf16[4,4096,64]{1,2,0:T(8,128)(2,1)} %fusion.23) | data formatting | bytes 4194304 | tf_op jit(solution)/shard_map/reshape | solution.py:92
  92.8 5.0 %fusion.13 = (f32[4,64,64]{2,1,0:T(8,128)S(1)}, f32[4,64,64,64]{2,3,1,0:T(8,128)S(1)}) fusion(pred[64,64]{1,0:T(8,128)(4,1)S(1)} %get-tuple-element.15, bf16[4,64,64,64]{3,2,1,0:T(8,128)(2,1)} %bitcast.158, bf16[4,64,64,64]{3,2,1,0:T(8,128)(2,1)} %bitcast.157), kind=kOutput, calls=%fused_computation.16 | convolution fusion | flops 137347072 | bytes 8458240 | tf_op jit(solution)/shard_map/huqe,huke->huqk/dot_general | solution.py:100
  97.8 5.3 %fusion.10 = bf16[64,64,64,4]{2,1,0,3:T(8,128)(2,1)S(1)} fusion(f32[64,64,4]{1,0,2:T(8,128)S(1)} %bitcast.187, bf16[4,64,64,64]{3,2,1,0:T(8,128)(2,1)S(1)} %bitcast.159, f32[4,64,64,64]{2,3,1,0:T(8,128)S(1)} %get-tuple-element.17, pred[64,64]{1,0:T(8,128)(4,1)S(1)} %get-tuple-element.15), kind=kOutput, calls=%fused_computation.13 | convolution fusion | flops 139460608 | bytes 8458240 | tf_op jit(solution)/shard_map/huqk,huke->huqe/dot_general | solution.py:108
  103.1 2.8 %convolution_bitcast_fusion = f32[4096,256]{1,0:T(8,128)} fusion(bf16[4096,64,4]{1,0,2:T(8,128)(2,1)S(1)} %bitcast.156, bf16[4,64,256]{2,1,0:T(8,128)(2,1)S(1)} %reshape_reshape_reshape.3), kind=kOutput, calls=%fused_computation.19 | convolution fusion | flops 536870912 | bytes 6422528 | tf_op jit(solution)/shard_map/huqe,hef->uqf/dot_general | solution.py:116
  105.9 9.2 %fusion.15 = f32[4096,256]{1,0:T(8,128)} fusion(f32[4096,256]{1,0:T(8,128)} %convolution_bitcast_fusion, bf16[1024,256]{1,0:T(8,128)(2,1)} %reshape_reshape.3, bf16[4096,256]{1,0:T(8,128)(2,1)S(1)} %bitcast.153, bf16[256,1024]{0,1:T(8,128)(2,1)S(1)} %bitcast.179), kind=kOutput, calls=%fused_computation.20 | convolution fusion | flops 4333764608 | bytes 11534336 | tf_op jit(solution)/shard_map/dot_general | solution.py:122
  115.1 3.6 %fusion.20 = bf16[4096,256]{1,0:T(8,128)(2,1)S(1)} fusion(f32[4096,256]{1,0:T(8,128)} %fusion.15, bf16[4096,256]{1,0:T(8,128)(2,1)} %bitcast.154, bf16[256,256]{0,1:T(8,128)(2,1)S(1)} %bitcast.175), kind=kOutput, calls=%fused_computation.22 | convolution fusion | flops 538968064 | bytes 8519680 | tf_op jit(solution)/shard_map/dot_general | solution.py:126
  119.9 1.8 %convolution_add_fusion.2 = f32[64,4,64]{2,1,0:T(4,128)S(1)} fusion(bf16[64,64,256]{2,1,0:T(8,128)(2,1)S(1)} %bitcast.146, f32[64,4,256]{2,1,0:T(4,128)S(1)} %get-tuple-element.19, f32[64,4]{1,0:T(8,128)S(1)} %copy.145, f32[4,64]{1,0:T(4,128)S(1)} %get-tuple-element.12), kind=kOutput, calls=%fused_computation.38 | convolution fusion | flops 50413568 | bytes 2426880 | tf_op jit(solution)/shard_map/ukd,uld->ukl/dot_general | solution.py:48
  123.2 1.8 %convolution_add_fusion.1 = f32[64,4,64]{2,1,0:T(4,128)S(1)} fusion(f32[64,4,64]{2,1,0:T(4,128)S(1)} %convolution_add_fusion.2, bf16[64,64,256]{2,1,0:T(8,128)(2,1)S(1)} %bitcast.148, f32[64,4,256]{2,1,0:T(4,128)S(1)} %get-tuple-element.23, f32[64,4]{1,0:T(8,128)S(1)} %copy.148), kind=kOutput, calls=%fused_computation.37 | convolution fusion | flops 50413568 | bytes 2491392 | tf_op jit(solution)/shard_map/ukd,uld->ukl/dot_general | solution.py:48
  127.3 5.5 %all_to_all.42 = f32[2,1,32768]{2,1,0:T(1,128)S(1)} all-to-all(f32[2,1,32768]{2,1,0:T(1,128)S(1)} %reshape.259), channel_id=1, replica_groups=mesh['au'=8,'pa'=8,'dev'=2] {'dev'}, dimensions={0} | all-to-all | bytes 524288 | tf_op jit(solution)/shard_map/all_to_all | solution.py:133
  (89 shorter events, 30.7 us)
Async XLA Ops:
  6.5 34.6 %copy-start = (bf16[4096,256]{1,0:T(8,128)(2,1)S(1)}, bf16[4096,256]{1,0:T(8,128)(2,1)}, u32[]{:S(2)}) copy-start(bf16[4096,256]{1,0:T(8,128)(2,1)} %param.12) | copy-start | bytes 6291460
  8.3 26.1 %all-to-all-start.1 = ((s32[8,1,512]{2,1,0:T(1,128)}), s32[8,1,512]{2,1,0:T(1,128)S(1)}, u32[]{:S(2)}, u32[]{:S(2)}) async-start(s32[8,1,512]{2,1,0:T(1,128)} %reshape.257), calls=%async_computation.1 | async-start | bytes 32768 | tf_op jit(solution)/shard_map/all_to_all | solution.py:78
  14.5 43.6 %all-gather.3.cloned.1.call-start = ((), (), s32[]{:S(2)}) async-start(), calls=%async_computation.3 | async-start | bytes 2555904 | tf_op jit(solution)/shard_map/all_gather | solution.py:29
  14.5 7.7 %copy-start.7 = (s32[1024]{0:T(1024)S(1)}, s32[1024]{0:T(1024)}, u32[]{:S(2)}) copy-start(s32[1024]{0:T(1024)} %param.13) | copy-start | bytes 12292
  19.5 1.0 copy-start.4
  20.6 13.7 %copy-start.8 = (s32[4,64]{1,0:T(4,128)S(1)}, s32[4,64]{1,0:T(4,128)}, u32[]{:S(2)}) copy-start(s32[4,64]{1,0:T(4,128)} %param.14) | copy-start | bytes 3076
  34.4 34.9 %all-to-all-start = ((bf16[8,64,8,256]{3,2,1,0:T(8,128)(2,1)}), bf16[8,64,8,256]{3,2,1,0:T(8,128)(2,1)}, u32[]{:S(2)}, u32[]{:S(2)}) async-start(bf16[8,64,8,256]{3,2,1,0:T(8,128)(2,1)} %fusion.36), calls=%async_computation | async-start | bytes 4194304 | tf_op jit(solution)/shard_map/all_to_all | solution.py:11
  69.3 2.8 %copy-start.6 = (bf16[1,256,2,128]{1,3,2,0:T(8,128)(2,1)S(1)}, bf16[1,256,2,128]{1,3,2,0:T(8,128)(2,1)}, u32[]{:S(2)}) copy-start(bf16[1,256,2,128]{1,3,2,0:T(8,128)(2,1)} %copy.134) | copy-start | bytes 393220
  72.1 33.8 %copy-start.2 = (bf16[64,8,8,256]{3,2,1,0:T(8,128)(2,1)}, bf16[64,8,8,256]{3,2,1,0:T(8,128)(2,1)S(1)}, u32[]{:S(2)}) copy-start(bf16[64,8,8,256]{3,2,1,0:T(8,128)(2,1)S(1)} %fusion.26) | copy-start | bytes 6291460
  74.2 4.8 %copy-start.5 = (bf16[1,256,2,128]{1,3,2,0:T(8,128)(2,1)S(1)}, bf16[1,256,2,128]{1,3,2,0:T(8,128)(2,1)}, u32[]{:S(2)}) copy-start(bf16[1,256,2,128]{1,3,2,0:T(8,128)(2,1)} %copy.129) | copy-start | bytes 393220
  92.8 5.0 %copy-start.3 = (bf16[4,4096,64]{2,1,0:T(8,128)(2,1)S(1)}, bf16[4,4096,64]{2,1,0:T(8,128)(2,1)}, u32[]{:S(2)}) copy-start(bf16[4,4096,64]{2,1,0:T(8,128)(2,1)} %copy.158) | copy-start | bytes 6291460
  126.4 9.7 %copy-start.1 = (bf16[4096,256]{1,0:T(8,128)(2,1)S(1)}, bf16[4096,256]{1,0:T(8,128)(2,1)}, u32[]{:S(2)}) copy-start(bf16[4096,256]{1,0:T(8,128)(2,1)} %param.12) | copy-start | bytes 6291460
Sparse Core Ops, SparseCore 0:
  20.7 15.7 all-gather.2
